TPU v7x, 1024 devices: a whole 4x8x16 slice. The times are simulated.
1024 devices in a mesh: seq: 16 (over y_hi, x, core), zero: 64 (over z, y_lo).
Axes of the slice: x: 4, y: 8 (y_hi: 2, y_lo: 4; y = y_hi * 4 + y_lo), z: 16, core: 2. Of those that a mesh axis runs over, the one named last changes fastest.
Arguments:
- inputs: bfloat16 [64, 4096, 1024], P('zero', 'seq'), may hold values from -16 to 16
- queries: bfloat16 [64, 4096, 512], P('zero', 'seq'), may hold values from -6 to 6
- values: bfloat16 [64, 4096, 512], P('zero', 'seq'), may hold values from -6 to 6
- w_key: bfloat16 [1024, 512], P('zero'), may hold values from -0.1875 to 0.1875
- state_in: float32 [64, 4, 128, 128], P('zero'), may hold values from -96 to 96
- norm_in: float32 [64, 4, 128], P('zero'), may hold values from 0.125 to 2048
- out_gain: float32 [512], replicated, may hold values from 0.5 to 1.5
- out_grad: bfloat16 [64, 4096, 512], P('zero', 'seq'), may hold values from -6 to 6
Outputs:
- attended: bfloat16 [64, 4096, 512], P('zero', 'seq')
- inputs_grad: bfloat16 [64, 4096, 1024], P('zero', 'seq')
- queries_grad: bfloat16 [64, 4096, 512], P('zero', 'seq')
- values_grad: bfloat16 [64, 4096, 512], P('zero', 'seq')
- w_key_grad: float32 [1024, 512], P(('seq', 'zero'))
All inputs are finite; a program needn't handle non-finite values.
Results may differ from a plain program's by a relative error of at most 0.015.
Values may be sent and summed in bfloat16 or wider, within the bound.
A program may use at most 64 MiB of HBM per device.

v0:
```python
import jax
import jax.numpy as jnp
from jax import lax
from jax.sharding import PartitionSpec as P

highest = lax.Precision.HIGHEST
epsilon = 1e-06


def entering(value, axis, combine, identity):
    devices, here = (lax.axis_size(axis), lax.axis_index(axis))
    everything = jax.tree.map(
        lambda part, kind: lax.all_gather(part.astype(kind), axis),
        value,
        (jnp.bfloat16, jnp.bfloat16),
    )
    start = jax.tree.map(
        lambda part, zero: jnp.broadcast_to(jnp.asarray(zero, part.dtype), part.shape),
        value,
        identity,
    )

    def turn(k, before):
        reached = k < here
        new = combine(
            before, jax.tree.map(lambda part, own: part[k].astype(own.dtype), everything, value)
        )
        return jax.tree.map(lambda a, b: jnp.where(reached, a, b), new, before)

    return lax.fori_loop(0, devices, turn, start)


def entering_2(value, axis, join, neutral):
    count = lax.axis_size(axis)
    place = lax.axis_index(axis)
    ahead = count - 1 - place
    gathered = jax.tree.map(
        lambda a, kind: lax.all_gather(a.astype(kind), axis),
        value,
        jax.tree.map(lambda a: jnp.bfloat16 if a.dtype == jnp.float32 else a.dtype, value),
    )
    state = jax.tree.map(lambda a, e: jnp.zeros_like(a) + jnp.asarray(e, a.dtype), value, neutral)

    def one(turn, state):
        source = count - 1 - turn
        return join(
            state,
            jax.tree.map(
                lambda a, own: lax.dynamic_index_in_dim(a, source, 0, False).astype(own.dtype),
                gathered,
                value,
            ),
        )

    return lax.fori_loop(0, ahead, one, state)


def feature(inner_values):
    return jax.nn.elu(inner_values) + 1.0


def slope(inner_values):
    return jnp.where(inner_values > 0, 1.0, jnp.exp(jnp.minimum(inner_values, 0.0)))


def add_pair(earlier, later):
    return (earlier[0] + later[0], earlier[1] + later[1])


def times_transposed(left, right):
    return lax.dot_general(
        left, right, (((1,), (1,)), ((), ())), preferred_element_type=jnp.float32
    )


def shards(inputs, queries, values, w_key, state_in, norm_in, out_gain, out_grad):
    full_key = lax.all_gather(w_key, "zero", axis=0, tiled=True)
    doc_count, tokens, model_width = inputs.shape
    head_count, head_size = (state_in.shape[1], state_in.shape[2])
    inner_width = head_count * head_size
    shape = (doc_count, tokens, head_count, head_size)
    token_rows = inputs.reshape(doc_count * tokens, model_width)
    key_lin = jnp.dot(token_rows, full_key, preferred_element_type=jnp.float32)
    feat_key = feature(key_lin).astype(jnp.bfloat16).reshape(shape)
    query_lin = queries.reshape(doc_count * tokens, inner_width).astype(jnp.float32)
    feat_query = feature(query_lin).astype(jnp.bfloat16).reshape(shape)
    values_b = values.reshape(shape)
    query_f = feat_query.astype(jnp.float32)
    keys_f = feat_key.astype(jnp.float32)
    block_kv = jnp.einsum("bthd,bthe->bhde", feat_key, values_b, preferred_element_type=jnp.float32)
    block_z = jnp.sum(keys_f, axis=1)
    prior_kv, prior_z = entering(
        (block_kv, block_z), "seq", add_pair, (jnp.zeros_like(block_kv), jnp.zeros_like(block_z))
    )
    state_now = state_in + prior_kv
    norm_now = norm_in + prior_z
    causal = jnp.arange(tokens)[:, None] >= jnp.arange(tokens)[None, :]
    scores = jnp.einsum("bthd,bshd->bhts", feat_query, feat_key, preferred_element_type=jnp.float32)
    weights = jnp.where(causal, scores, 0.0).astype(jnp.bfloat16)
    numerator = jnp.einsum("bhts,bshe->bthe", weights, values_b, preferred_element_type=jnp.float32)
    numerator = numerator + jnp.einsum("bthd,bhde->bthe", query_f, state_now, precision=highest)
    denominator = jnp.transpose(jnp.sum(weights.astype(jnp.float32), axis=-1), (0, 2, 1))
    denominator = denominator + jnp.einsum("bthd,bhd->bth", query_f, norm_now, precision=highest)
    head_out = numerator / denominator[..., None]
    flat_out = head_out.reshape(doc_count, tokens, inner_width)
    inv_rms = lax.rsqrt(jnp.mean(flat_out * flat_out, axis=-1, keepdims=True) + epsilon)
    attended = (flat_out * inv_rms * out_gain).astype(jnp.bfloat16)
    scaled = out_grad.astype(jnp.float32) * out_gain
    inner = jnp.mean(scaled * flat_out, axis=-1, keepdims=True)
    d_head = (inv_rms * (scaled - flat_out * inner * inv_rms * inv_rms)).reshape(shape)
    grad_num = (d_head / denominator[..., None]).astype(jnp.bfloat16)
    grad_num_f = lax.optimization_barrier(grad_num).astype(jnp.float32)
    grad_den = -jnp.sum(d_head * head_out, axis=-1) / denominator
    d_weights = jnp.einsum(
        "bthe,bshe->bhts", grad_num, values_b, preferred_element_type=jnp.float32
    )
    d_weights = d_weights + jnp.transpose(grad_den, (0, 2, 1))[..., None]
    d_weights = jnp.where(causal, d_weights, 0.0).astype(jnp.bfloat16)
    ds_local = jnp.einsum(
        "bthd,bthe->bhde", feat_query, grad_num, preferred_element_type=jnp.float32
    )
    dz_local = jnp.einsum("bth,bthd->bhd", grad_den, query_f, precision=highest)
    carry_s, carry_z = entering_2(
        (ds_local, dz_local), "seq", add_pair, (jnp.zeros_like(ds_local), jnp.zeros_like(dz_local))
    )
    d_feat_key = jnp.einsum(
        "bhts,bthd->bshd", d_weights, feat_query, preferred_element_type=jnp.float32
    )
    d_feat_key = d_feat_key + jnp.einsum(
        "bshe,bhde->bshd", values_b.astype(jnp.float32), carry_s, precision=highest
    )
    d_feat_key = d_feat_key + carry_z[:, None]
    d_value = jnp.einsum("bhts,bthe->bshe", weights, grad_num, preferred_element_type=jnp.float32)
    d_value = d_value + jnp.einsum("bshd,bhde->bshe", keys_f, carry_s, precision=highest)
    d_feat_query = jnp.einsum(
        "bhts,bshd->bthd", d_weights, feat_key, preferred_element_type=jnp.float32
    )
    d_feat_query = d_feat_query + jnp.einsum(
        "bthe,bhde->bthd", grad_num_f, state_now, precision=highest
    )
    d_feat_query = d_feat_query + grad_den[..., None] * norm_now[:, None]
    flat_rows = doc_count * tokens
    d_key = (d_feat_key.reshape(flat_rows, inner_width) * slope(key_lin)).astype(jnp.bfloat16)
    values_grad = d_value.reshape(doc_count, tokens, inner_width).astype(jnp.bfloat16)
    queries_grad = (d_feat_query.reshape(flat_rows, inner_width) * slope(query_lin)).astype(
        jnp.bfloat16
    )
    inputs_grad = (
        times_transposed(d_key, full_key)
        .astype(jnp.bfloat16)
        .reshape(doc_count, tokens, model_width)
    )
    partial_sum = lax.psum_scatter(
        lax.dot_general(
            token_rows, d_key, (((0,), (0,)), ((), ())), preferred_element_type=jnp.float32
        ).astype(jnp.bfloat16),
        "seq",
        scatter_dimension=0,
        tiled=True,
    ).astype(jnp.float32)
    summed = lax.psum_scatter(partial_sum, "zero", scatter_dimension=0, tiled=True)
    return (
        attended,
        inputs_grad,
        queries_grad.reshape(doc_count, tokens, inner_width),
        values_grad,
        summed,
    )


def solution(mesh):
    return jax.shard_map(
        shards,
        mesh=mesh,
        in_specs=(
            P("zero", "seq", None),
            P("zero", "seq", None),
            P("zero", "seq", None),
            P("zero", None),
            P("zero", None, None, None),
            P("zero", None, None),
            P(),
            P("zero", "seq", None),
        ),
        out_specs=(
            P("zero", "seq", None),
            P("zero", "seq", None),
            P("zero", "seq", None),
            P("zero", "seq", None),
            P(("seq", "zero"), None),
        ),
        check_vma=False,
    )
```

profile of v0, /device:TPU:2, one launch (start us, length us, event | category | flops | bytes accessed | tf_op | source)
XLA Modules:
  0.0 916.1 jit_solution(12709292732950309564)
XLA Ops:
  8.0 1.0 reshape.433
  9.0 307.7 %all-gather.8.cloned.1.call-done = bf16[1024,512]{1,0:T(8,128)(2,1)} async-done(((bf16[16,512]{1,0:T(8,128)(2,1)}), bf16[1024,512]{1,0:T(8,128)(2,1)}) %all-gather.8.cloned.1.call-update) | async-done | bytes 1048592 | tf_op jit(solution)/shard_map/all_gather | solution.py:77
  316.7 2.5 fusion.41
  320.8 24.2 %all_gather.31 = bf16[16,1,4,128]{3,2,1,0:T(4,128)(2,1)S(1)} all-gather(bf16[1,1,4,128]{3,2,1,0:T(4,128)(2,1)S(1)} %bitcast.175), channel_id=1, replica_groups=mesh['seq'=16,'zero'=64] {'seq'}, dimensions={0}, use_global_device_ids=true | all-gather | bytes 17408 | tf_op jit(solution)/shard_map/all_gather | solution.py:13
  345.6 46.9 %all-gather.10.cloned.1.call-done = bf16[64,128,128]{2,1,0:T(8,128)(2,1)} async-done(((bf16[4,128,128]{2,1,0:T(8,128)(2,1)}), bf16[64,128,128]{2,1,0:T(8,128)(2,1)}) %all-gather.10.cloned.1.call-update) | async-done | bytes 2097168 | tf_op jit(solution)/shard_map/all_gather | solution.py:13
  392.5 17.3 %while.31 = (s32[]{:T(128)}, f32[1,4,128,128]{3,2,1,0:T(8,128)S(1)}, f32[1,4,128]{2,1,0:T(4,128)S(1)}, s32[]{:T(128)}, bf16[16,1,4,128,128]{4,3,2,1,0:T(8,128)(2...) while((s32[]{:T(128)}, f32[1,4,128,128]{3,2,1,0:T(8,128)S(1)}, ...), condition=%wide.region_2.3_spmd.clone, body=%wide.region_1.2_spmd.clone.sunk | while | flops 264196 | bytes 660603 | solution.py:30
  392.6 1.0 add_select_fusion.4
  393.6 1.0 add_select_fusion.4
  394.7 1.0 add_select_fusion.4
  395.8 1.0 add_select_fusion.4
  396.9 1.0 add_select_fusion.4
  398.0 1.0 add_select_fusion.4
  399.0 1.0 add_select_fusion.4
  400.1 1.0 add_select_fusion.4
  401.2 1.0 add_select_fusion.4
  402.3 1.0 add_select_fusion.4
  403.4 1.0 add_select_fusion.4
  404.5 1.0 add_select_fusion.4
  405.5 1.0 add_select_fusion.4
  406.6 1.0 add_select_fusion.4
  407.7 1.0 add_select_fusion.4
  408.8 1.0 add_select_fusion.4
  413.1 1.3 dynamic-slice
  414.8 26.6 %all-gather.3 = bf16[16,4,128]{2,1,0:T(4,128)(2,1)S(1)} all-gather(bf16[1,4,128]{2,1,0:T(4,128)(2,1)S(1)} %convert_bitcast_fusion), channel_id=4, replica_groups=mesh['seq'=16,'zero'=64] {'seq'}, dimensions={0}, use_global_device_ids=true | all-gather | bytes 17408 | tf_op jit(solution)/shard_map/all_gather | solution.py:38
  442.0 46.3 %all-gather.12.cloned.1.call-done = bf16[64,128,128]{2,1,0:T(8,128)(2,1)} async-done(((bf16[4,128,128]{2,1,0:T(8,128)(2,1)}), bf16[64,128,128]{2,1,0:T(8,128)(2,1)}) %all-gather.12.cloned.1.call-update) | async-done | bytes 2097168 | tf_op jit(solution)/shard_map/all_gather | solution.py:38
  488.3 13.1 %while.30 = (s32[]{:T(128)}, f32[1,4,128,128]{3,2,1,0:T(8,128)S(1)}, f32[1,4,128]{2,1,0:T(4,128)S(1)}, s32[]{:T(128)}, bf16[16,1,4,128,128]{4,3,2,1,0:T(8,128)(2...) while((s32[]{:T(128)}, f32[1,4,128,128]{3,2,1,0:T(8,128)S(1)}, ...), condition=%wide.region_8.9_spmd, body=%wide.region_7.8_spmd.sunk | while | flops 132102 | bytes 660643 | solution.py:55
  488.4 1.0 convert_add_fusion.4
  489.4 1.0 convert_add_fusion.4
  490.4 1.0 convert_add_fusion.4
  491.4 1.0 convert_add_fusion.4
  492.4 1.0 convert_add_fusion.4
  493.4 1.0 convert_add_fusion.4
  494.4 1.0 convert_add_fusion.4
  495.4 1.0 convert_add_fusion.4
  496.4 1.0 convert_add_fusion.4
  497.4 1.0 convert_add_fusion.4
  498.4 1.0 convert_add_fusion.4
  499.4 1.0 convert_add_fusion.4
  500.4 1.0 convert_add_fusion.4
  502.0 1.2 fusion.16
  503.6 1.3 copy.100
  505.0 1.0 copy-done.4
  506.9 1.9 multiply_convert_fusion
  509.1 1.4 fusion.10
  511.3 1.3 fusion.4
  512.6 96.4 %reduce-scatter.5.cloned.1.call-done = bf16[64,512]{1,0:T(8,128)(2,1)} async-done(((bf16[1024,512]{1,0:T(8,128)(2,1)}), bf16[64,512]{1,0:T(8,128)(2,1)}) %reduce-scatter.5.cloned.1.call-update) | async-done | bytes 65552
  608.9 1.0 copy.101
  609.9 298.3 %all-reduce.2 = f32[64,512]{0,1:T(8,128)S(1)} all-reduce(bf16[64,512]{0,1:T(8,128)(2,1)S(1)} %copy.101), channel_id=6, replica_groups=mesh['seq'=16,'zero'=64] {'zero'}, use_global_device_ids=true, to_apply=%region_10.11.clone | all-reduce | flops 32768 | bytes 196608
  (101 shorter events, 12.0 us)
Async XLA Ops:
  7.2 309.6 %copy-start = (bf16[1,256,1024]{2,1,0:T(8,128)(2,1)S(1)}, bf16[1,256,1024]{2,1,0:T(8,128)(2,1)}, u32[]{:S(2)}) copy-start(bf16[1,256,1024]{2,1,0:T(8,128)(2,1)} %param.12) | copy-start | bytes 1572868
  7.2 309.5 %all-gather.8.cloned.1.call-start = ((), (), s32[]{:S(2)}) async-start(), calls=%async_computation.1 | async-start | bytes 1064960 | tf_op jit(solution)/shard_map/all_gather | solution.py:77
  7.9 384.6 %all-gather.10.cloned.1.call-start = ((), (), s32[]{:S(2)}) async-start(), calls=%async_computation.2 | async-start | bytes 2228224 | tf_op jit(solution)/shard_map/all_gather | solution.py:13
  9.0 311.4 %copy-start.7 = (bf16[1,256,512]{2,1,0:T(8,128)(2,1)S(1)}, bf16[1,256,512]{2,1,0:T(8,128)(2,1)}, u32[]{:S(2)}) copy-start(bf16[1,256,512]{2,1,0:T(8,128)(2,1)} %param.13) | copy-start | bytes 786436
  319.3 26.0 %copy-start.6 = (bf16[256,512]{1,0:T(8,128)(2,1)}, bf16[256,512]{1,0:T(8,128)(2,1)S(1)}, u32[]{:S(2)}) copy-start(bf16[256,512]{1,0:T(8,128)(2,1)S(1)} %get-tuple-element.280) | copy-start | bytes 786436
  320.3 168.0 %all-gather.12.cloned.1.call-start = ((), (), s32[]{:S(2)}) async-start(), calls=%async_computation.3 | async-start | bytes 2228224 | tf_op jit(solution)/shard_map/all_gather | solution.py:38
  345.3 47.2 %copy-start.1 = (bf16[4,256,256]{1,2,0:T(8,128)(2,1)}, bf16[4,256,256]{1,2,0:T(8,128)(2,1)S(1)}, u32[]{:S(2)}) copy-start(bf16[4,256,256]{1,2,0:T(8,128)(2,1)S(1)} %get-tuple-element.285) | copy-start | bytes 1572868
  345.3 64.6 %copy-start.12 = (f32[1,4,128]{2,1,0:T(4,128)S(1)}, f32[1,4,128]{2,1,0:T(4,128)}, u32[]{:S(2)}) copy-start(f32[1,4,128]{2,1,0:T(4,128)} %param.17) | copy-start | bytes 6148
  345.6 64.5 %copy-start.9 = (f32[1,4,128,128]{3,2,1,0:T(8,128)S(1)}, f32[1,4,128,128]{3,2,1,0:T(8,128)}, u32[]{:S(2)}) copy-start(f32[1,4,128,128]{3,2,1,0:T(8,128)} %param.16) | copy-start | bytes 786436
  409.8 1.0 copy-start.8
  409.9 1.0 copy-start.11
  413.1 195.9 %reduce-scatter.5.cloned.1.call-start = ((), (), s32[]{:S(2)}) async-start(), calls=%async_computation.4 | async-start | bytes 1114112
  441.7 46.6 %copy-start.3 = (bf16[4,256,256]{1,2,0:T(8,128)(2,1)}, bf16[4,256,256]{1,2,0:T(8,128)(2,1)S(1)}, u32[]{:S(2)}) copy-start(bf16[4,256,256]{1,2,0:T(8,128)(2,1)S(1)} %fusion.2) | copy-start | bytes 1572868
  505.0 1.0 copy-start.4
  505.0 1.3 copy-start.10
  506.2 2.5 copy-start.2
  506.9 4.4 copy-start.5
Sparse Core Ops, SparseCore 0:
  10.7 306.0 all-gather.7
  321.8 70.7 all-gather.9
  413.2 75.0 all-gather.11
  505.1 103.7 reduce-scatter.4
where the time goes:
time: 917 us; the launch traced here: 916 us
  waiting for transfers between devices  498 us (54%)
  blocking collectives  349 us (38%)
  other arithmetic  34.3 us (4%)
  between operations  14.1 us (2%)
  matrix products  10.9 us (1%)
    all_gather x1, waiting for transfers between devices, shards(): full_key = lax.all_gather(w_key, 'zero', axis=0, tiled=True)  308 us
    unnamed x1, blocking collectives  298 us
    unnamed x5, waiting for transfers between devices  97.1 us
    all_gather x1, waiting for transfers between devices, entering(): lax.all_gather(part.astype(kind), axis)  46.9 us
    all_gather x1, waiting for transfers between devices, entering_2(): lax.all_gather(a.astype(kind), axis)  46.3 us
    all_gather x1, blocking collectives, entering_2(): lax.all_gather(a.astype(kind), axis)  26.6 us
    all_gather x1, blocking collectives, entering(): lax.all_gather(part.astype(kind), axis)  24.2 us
  transfers between devices with their start and end apart: 4, of which 4 were waited for; matrix products, arithmetic and copies ran while one was open for 1% of the time, Pallas kernels for 0%

commit v1 on v0

v1 whole, which is shorter than its diff:
```python
import jax
import jax.numpy as jnp
from jax import lax
from jax.experimental import pallas as pl
from jax.experimental.pallas import tpu as pltpu
from jax.sharding import PartitionSpec as P

epsilon = 1e-06
MESH = pl.DeviceIdType.MESH
F32 = jnp.float32
BF16 = jnp.bfloat16

Y_HI, X, CORES = 2, 4, 2
Z, Y_LO = 16, 4
GROUP = X * CORES
RING_Y = Y_HI * Y_LO
HEADS, HEAD = 4, 128
WIDTH = HEADS * HEAD


def dot(a, b):
    return jnp.dot(a, b, preferred_element_type=F32)


def dot_nt(a, b):
    return lax.dot_general(a, b, (((1,), (1,)), ((), ())), preferred_element_type=F32)


def dot_tn(a, b):
    return lax.dot_general(a, b, (((0,), (0,)), ((), ())), preferred_element_type=F32)


def wide(value):
    return value.astype(F32)


def features(value):
    low = jnp.exp(jnp.minimum(value, 0.0))
    positive = value > 0
    return jnp.where(positive, value + 1.0, low), jnp.where(positive, 1.0, low)


def body(
    inp, q, v, w, st, nm, gain, og,
    att, ig, qg, vg, wg,
    wf, inpt, fq, slq, fk, slk, wts, numi, deni, ho, rec, gn, gd, state, dfk, dval, dk, norm,
    f_out, f_in, f_tot, f_tot_in, f_pre, f_ret,
    b_out, b_in, b_tot, b_tot_in, b_pre, b_ret,
    gown, gsend, grecv, xsend, xrecv, ykeep, ysend, yrecv, zsend, zrecv,
    local_sem,
    wz_s, wz_r, wy_s, wy_r, wx_s, wx_r, wc_s, wc_r,
    fa_s, fa_r, fy_s, fy_r, fb_s, fb_r,
    ba_s, ba_r, by_s, by_r, bb_s, bb_r,
    rc_s, rc_r, rx_s, rx_r, ry_s, ry_r, rz_s, rz_r,
):
    seq, zero = lax.axis_index("seq"), lax.axis_index("zero")
    core = lax.rem(seq, CORES)
    x = lax.rem(seq // CORES, X)
    y_hi = seq // GROUP
    z = zero // Y_LO
    y_lo = lax.rem(zero, Y_LO)
    y = y_hi * Y_LO + y_lo
    own = x * CORES + core
    partner = seq + 1 - 2 * core
    tokens, model = inp.shape
    depth = w.shape[0]
    half = depth // CORES
    block = WIDTH // X

    def send(source, target, s_sem, r_sem, to_seq, to_zero):
        return pltpu.make_async_remote_copy(
            src_ref=source,
            dst_ref=target,
            send_sem=s_sem,
            recv_sem=r_sem,
            device_id={"seq": to_seq, "zero": to_zero},
            device_id_type=MESH,
        )

    def along_z(k):
        return seq, lax.rem(z + k, Z) * Y_LO + y_lo

    def along_y(k):
        there = lax.rem(y + k + RING_Y, RING_Y)
        return (
            (there // Y_LO) * GROUP + own,
            z * Y_LO + lax.rem(there, Y_LO),
        )

    def along_x(k):
        return y_hi * GROUP + lax.rem(x + k, X) * CORES + core, zero

    def in_group(k):
        return y_hi * GROUP + lax.rem(own + k, GROUP), zero

    barrier = pltpu.get_barrier_semaphore()

    def greet(place):
        pl.semaphore_signal(
            barrier, inc=1, device_id={"seq": place[0], "zero": place[1]}, device_id_type=MESH
        )

    def greet_z(k, carry):
        greet(along_z(k))
        return carry

    lax.fori_loop(1, Z, greet_z, 0)
    for k in range(1, RING_Y):
        greet(along_y(k))
    for k in range(1, GROUP):
        greet(in_group(k))
    pl.semaphore_wait(barrier, Z + RING_Y + GROUP - 3)

    sent = []

    def rows_of(c):
        return pl.ds(pl.multiple_of(c * half, half), half)

    def columns_of(xx):
        return pl.ds(pl.multiple_of(xx * block, block), block)

    rows, columns = rows_of(core), columns_of(x)

    def z_copy(k):
        return send(
            w.at[rows, columns], wf.at[z, y_lo, rows, columns],
            wz_s.at[k - 1], wz_r.at[k - 1], *along_z(k),
        )

    def z_arrival(k):
        origin = lax.rem(z - k + Z, Z)
        return send(
            w.at[rows, columns], wf.at[origin, y_lo, rows, columns],
            wz_s.at[k - 1], wz_r.at[k - 1], *along_z(k),
        )

    def far_first(n):
        return Z // 2 + ((n + 1) // 2) * (1 - 2 * lax.rem(n, 2))

    def z_start(n, carry):
        z_copy(far_first(n)).start()
        return carry

    lax.fori_loop(0, Z - 1, z_start, 0)
    keep = pltpu.make_async_copy(
        w.at[rows, columns], wf.at[z, y_lo, rows, columns], local_sem.at[0]
    )
    keep.start()

    span = CORES * Z * Y_LO
    j = lax.broadcasted_iota(jnp.int32, (span, span), 0)
    i = lax.broadcasted_iota(jnp.int32, (span, span), 1)
    within = lax.rem(j, Z * Y_LO)
    source = (j - within) + lax.rem(within, Z) * Y_LO + within // Z
    pick = jnp.where(source == i, 1.0, 0.0).astype(BF16)
    for b in range(Y_HI * X):
        turned = dot_nt(pick, inp[:, b * span : (b + 1) * span]).astype(BF16)
        for c in range(CORES):
            inpt[b // X, b % X, c] = turned[c * (span // CORES) : (c + 1) * (span // CORES)]
    for h in range(HEADS):
        lanes = slice(h * HEAD, (h + 1) * HEAD)
        feat, slope = features(wide(q[:, lanes]))
        fq[:, lanes] = feat.astype(BF16)
        slq[:, lanes] = slope

    def z_wait(k, carry):
        z_arrival(k).wait_recv()
        return carry

    keep.wait()
    lax.fori_loop(1, Z, z_wait, 0)

    steps_y = [1, -1, 2 - 4 * core] if Y_LO == 4 else [1]

    def piece(n, k, r):
        lo = y_lo if n == 0 else lax.rem(y_lo - steps_y[n - 1] + 2 * Y_LO, Y_LO)
        return wf.at[:, lo, r, columns_of(lax.rem(x - k + X, X))]

    def y_copy(n, at):
        return send(at, at, wy_s.at[n], wy_r.at[n], *along_y(steps_y[n]))

    def x_copy(n, k, at):
        slot = n * (X - 1) + k - 1
        return send(at, at, wx_s.at[slot], wx_r.at[slot], *along_x(k))

    def c_copy(n, k, at):
        slot = n * X + k
        return send(at, at, wc_s.at[slot], wc_r.at[slot], partner, zero)

    def pass_on(n):
        at = piece(n, 0, rows)
        for k in (2, 1, 3) if X == 4 else range(1, X):
            copy = x_copy(n, k, at)
            copy.start()
            sent.append(copy)
        copy = c_copy(n, 0, at)
        copy.start()
        sent.append(copy)

    for n in range(len(steps_y)):
        copy = y_copy(n, piece(0, 0, rows))
        copy.start()
        sent.append(copy)
    pass_on(0)
    for n in range(len(steps_y)):
        y_copy(n, piece(n + 1, 0, rows)).wait_recv()
        pass_on(n + 1)
    for n in range(Y_LO):
        for k in range(1, X):
            at = piece(n, k, rows)
            x_copy(n, k, at).wait_recv()
            copy = c_copy(n, k, at)
            copy.start()
            sent.append(copy)
    other_rows = rows_of(1 - core)
    for n in range(Y_LO):
        for k in range(X):
            c_copy(n, k, piece(n, k, other_rows)).wait_recv()

    for h in range(HEADS):
        lanes = slice(h * HEAD, (h + 1) * HEAD)
        weight = wf[:, :, :, lanes].reshape(model, HEAD)
        feat, slope = features(dot(inp[...], weight))
        fk[:, lanes] = feat.astype(BF16)
        slk[:, lanes] = slope

    part = WIDTH // GROUP
    padded = f_out.shape[1]

    def scan_start(mats, sums, out, inside, s_sem, r_sem):
        per = HEAD // part if part <= HEAD else 1
        for h in range(HEADS):
            for p in range(per):
                slot = h * per + p
                out[slot, 0:part] = mats[h][p * part : (p + 1) * part].astype(BF16)
                out[slot, part:padded] = jnp.broadcast_to(sums[h], (padded - part, HEAD)).astype(
                    BF16
                )
        for k in range(1, GROUP):
            copy = send(
                out.at[lax.rem(own + k, GROUP)], inside.at[own],
                s_sem.at[k - 1], r_sem.at[k - 1], *in_group(k),
            )
            copy.start()
            sent.append(copy)
        inside[pl.ds(own, 1)] = out[pl.ds(own, 1)]

    def group_wait(buffer, s_sem, r_sem):
        for k in range(1, GROUP):
            at = buffer.at[lax.rem(own - k + GROUP, GROUP)]
            send(at, at, s_sem.at[k - 1], r_sem.at[k - 1], *in_group(k)).wait_recv()

    def scan_total(out, inside, total, total_in, s_sem, r_sem, y_s, y_r):
        group_wait(inside, s_sem, r_sem)
        running = wide(inside[0])
        for p in range(1, GROUP):
            running = running + wide(inside[p])
        total[...] = running.astype(BF16)
        copy = send(total, total_in, y_s.at[0], y_r.at[0], *along_y(Y_LO))
        copy.start()
        sent.append(copy)
        return copy

    def scan_back(inside, total_in, copy, taken, order, pre, ret, s_sem, r_sem):
        copy.wait_recv()
        running = wide(total_in[...]) * taken.astype(F32)
        for p in order:
            pre[p] = running.astype(BF16)
            running = running + wide(inside[p])
        for k in range(1, GROUP):
            copy = send(
                pre.at[lax.rem(own + k, GROUP)], ret.at[own],
                s_sem.at[k - 1], r_sem.at[k - 1], *in_group(k),
            )
            copy.start()
            sent.append(copy)
        ret[pl.ds(own, 1)] = pre[pl.ds(own, 1)]

    def scan_result(ret, h):
        per = HEAD // part
        mats = [ret[h * per + p, 0:part] for p in range(per)]
        mat = mats[0] if per == 1 else jnp.concatenate(mats, axis=0)
        return mat, wide(ret[h * per, part : part + 16])[0:1]

    mats, sums = [], []
    for h in range(HEADS):
        lanes = slice(h * HEAD, (h + 1) * HEAD)
        mats.append(dot_tn(fk[:, lanes], v[:, lanes]))
        sums.append(jnp.sum(wide(fk[:, lanes]), axis=0, keepdims=True))
    scan_start(mats, sums, f_out, f_in, fa_s, fa_r)

    causal = lax.broadcasted_iota(jnp.int32, (tokens, tokens), 0) >= lax.broadcasted_iota(
        jnp.int32, (tokens, tokens), 1
    )

    def inside_block(h):
        lanes = slice(h * HEAD, (h + 1) * HEAD)
        scores = dot_nt(fq[:, lanes], fk[:, lanes])
        weights = jnp.where(causal, scores, 0.0).astype(BF16)
        wts[h] = weights
        extended = jnp.concatenate([v[:, lanes], jnp.ones((tokens, HEAD), BF16)], axis=1)
        both = dot(weights, extended)
        numi[:, lanes] = both[:, :HEAD]
        deni[:, lanes] = both[:, HEAD:]

    for h in range(HEADS // 2):
        inside_block(h)
    swap = scan_total(f_out, f_in, f_tot, f_tot_in, fa_s, fa_r, fy_s, fy_r)
    for h in range(HEADS // 2, HEADS):
        inside_block(h)
    scan_back(f_in, f_tot_in, swap, y_hi, range(GROUP), f_pre, f_ret, fb_s, fb_r)
    group_wait(f_ret, fb_s, fb_r)

    squares = jnp.zeros((tokens, HEAD), F32)
    crossed = jnp.zeros((tokens, HEAD), F32)
    for h in range(HEADS):
        lanes = slice(h * HEAD, (h + 1) * HEAD)
        prior, prior_sum = scan_result(f_ret, h)
        now = (st[h] + wide(prior)).astype(BF16)
        norm_now = nm[h : h + 1] + prior_sum
        state[h] = now
        norm[h] = norm_now
        query = fq[:, lanes]
        numerator = numi[:, lanes] + dot(query, now)
        denominator = deni[:, lanes] + jnp.sum(wide(query) * norm_now, axis=1, keepdims=True)
        inverse = 1.0 / denominator
        out = numerator * inverse
        ho[:, lanes] = out
        rec[:, lanes] = inverse
        squares = squares + out * out
        crossed = crossed + wide(og[:, lanes]) * gain[:, lanes] * out
    inv_rms = lax.rsqrt(jnp.sum(squares, axis=1, keepdims=True) / WIDTH + epsilon)
    inner = jnp.sum(crossed, axis=1, keepdims=True) / WIDTH
    factor = inner * inv_rms * inv_rms
    mats, sums = [], []
    for h in range(HEADS):
        lanes = slice(h * HEAD, (h + 1) * HEAD)
        out = ho[:, lanes]
        d_head = inv_rms * (wide(og[:, lanes]) * gain[:, lanes] - out * factor)
        numerator_grad = (d_head * rec[:, lanes]).astype(BF16)
        denominator_grad = -jnp.sum(d_head * out, axis=1, keepdims=True) * rec[:, lanes]
        gn[:, lanes] = numerator_grad
        gd[:, lanes] = denominator_grad
        mats.append(dot_tn(fq[:, lanes], numerator_grad))
        sums.append(jnp.sum(denominator_grad * wide(fq[:, lanes]), axis=0, keepdims=True))
    scan_start(mats, sums, b_out, b_in, ba_s, ba_r)

    def block_grads(h):
        lanes = slice(h * HEAD, (h + 1) * HEAD)
        grad = gn[:, lanes]
        row_grad = gd[:, lanes]
        d_weights = dot_nt(grad, v[:, lanes]) + jnp.concatenate(
            [row_grad] * (tokens // HEAD), axis=1
        )
        d_weights = jnp.where(causal, d_weights, 0.0).astype(BF16)
        dfk[:, lanes] = dot_tn(d_weights, fq[:, lanes])
        dval[:, lanes] = dot_tn(wts[h], grad)
        d_query = dot(d_weights, fk[:, lanes]) + dot_nt(grad, state[h]) + row_grad * norm[h]
        qg[:, lanes] = (d_query * slq[:, lanes]).astype(BF16)

    for h in range(HEADS // 2):
        block_grads(h)
    swap = scan_total(b_out, b_in, b_tot, b_tot_in, ba_s, ba_r, by_s, by_r)
    for h in range(HEADS // 2, HEADS):
        block_grads(h)
    scan_back(
        b_in, b_tot_in, swap, 1 - y_hi, range(GROUP - 1, -1, -1), b_pre, b_ret, bb_s, bb_r
    )
    for h in range(HEADS):
        lanes = slice(h * HEAD, (h + 1) * HEAD)
        att[:, lanes] = (ho[:, lanes] * inv_rms * gain[:, lanes]).astype(BF16)
    group_wait(b_ret, bb_s, bb_r)
    for h in range(HEADS):
        lanes = slice(h * HEAD, (h + 1) * HEAD)
        carry, carry_sum = scan_result(b_ret, h)
        total = dfk[:, lanes] + dot_nt(v[:, lanes], carry) + carry_sum
        dk[:, lanes] = (total * slk[:, lanes]).astype(BF16)

    def partial_of(xx, c):
        left = jnp.concatenate([inpt[hi, xx, c] for hi in range(Y_HI)], axis=0)
        return dot(left, dk[...])

    order = (2, 1, 3, 0) if X == 4 else tuple(range(1, X)) + (0,)

    def rc_copy(k):
        return send(gsend.at[k], grecv.at[k], rc_s.at[k], rc_r.at[k], partner, zero)

    for k in order:
        gsend[k] = partial_of(lax.rem(x + k, X), 1 - core).astype(BF16)
        copy = rc_copy(k)
        copy.start()
        sent.append(copy)
    for k in order:
        gown[k] = partial_of(lax.rem(x + k, X), core)

    def rx_copy(k):
        return send(
            xsend.at[k - 1], xrecv.at[k - 1], rx_s.at[k - 1], rx_r.at[k - 1], *along_x(k)
        )

    for k in order:
        rc_copy(k).wait_recv()
        if k:
            xsend[k - 1] = (gown[k] + wide(grecv[k])).astype(BF16)
            copy = rx_copy(k)
            copy.start()
            sent.append(copy)

    for h in range(HEADS):
        lanes = slice(h * HEAD, (h + 1) * HEAD)
        carry, _ = scan_result(b_ret, h)
        vg[:, lanes] = (dval[:, lanes] + dot(fk[:, lanes], carry)).astype(BF16)
    ig[...] = dot_nt(dk[...], wf[...].reshape(model, WIDTH)).astype(BF16)

    for k in range(1, X):
        rx_copy(k).wait_recv()
    total = gown[0] + wide(grecv[0])
    for k in range(1, X):
        total = total + wide(xrecv[k - 1])
    for there in range(RING_Y):
        part_y = total[there * Z : (there + 1) * Z]
        ykeep[there] = part_y
        ysend[there] = part_y.astype(BF16)

    def ry_copy(k):
        return send(
            ysend.at[lax.rem(y + k, RING_Y)], yrecv.at[k - 1],
            ry_s.at[k - 1], ry_r.at[k - 1], *along_y(k),
        )

    for k in (4, 3, 5, 2, 6, 1, 7) if RING_Y == 8 else range(1, RING_Y):
        copy = ry_copy(k)
        copy.start()
        sent.append(copy)
    total = ykeep[pl.ds(y, 1)][0]
    for k in range(1, RING_Y):
        ry_copy(k).wait_recv()
        total = total + wide(yrecv[k - 1])
    zsend[:, 0, :] = total

    def rz_copy(k):
        return send(
            zsend.at[lax.rem(z + k, Z)], zrecv.at[k - 1],
            rz_s.at[k - 1], rz_r.at[k - 1], *along_z(k),
        )

    def rz_start(n, carry):
        rz_copy(far_first(n)).start()
        return carry

    lax.fori_loop(0, Z - 1, rz_start, 0)
    last = zsend[pl.ds(z, 1)][0]
    for k in range(1, Z):
        rz_copy(k).wait_recv()
        last = last + zrecv[k - 1]
    wg[...] = last

    for copy in sent:
        copy.wait_send()

    def z_sent(k, carry):
        z_copy(k).wait_send()
        rz_copy(k).wait_send()
        return carry

    lax.fori_loop(1, Z, z_sent, 0)


def shards(inputs, queries, values, w_key, state_in, norm_in, out_gain, out_grad):
    docs, tokens, model = inputs.shape
    depth = w_key.shape[0]
    part = WIDTH // GROUP
    padded = part + 16
    rows_out = Z * Y_LO
    dma = pltpu.SemaphoreType.DMA
    vmem = pltpu.VMEM
    scan_buffers = [
        vmem((GROUP, padded, HEAD), BF16),
        vmem((GROUP, padded, HEAD), BF16),
        vmem((padded, HEAD), BF16),
        vmem((padded, HEAD), BF16),
        vmem((GROUP, padded, HEAD), BF16),
        vmem((GROUP, padded, HEAD), BF16),
    ]
    scan_sems = [dma((GROUP - 1,))] * 2 + [dma((1,))] * 2 + [dma((GROUP - 1,))] * 2
    scratch = (
        [
            vmem((Z, Y_LO, depth, WIDTH), BF16),
            vmem((Y_HI, X, CORES, rows_out, tokens), BF16),
            vmem((tokens, WIDTH), BF16),
            vmem((tokens, WIDTH), F32),
            vmem((tokens, WIDTH), BF16),
            vmem((tokens, WIDTH), F32),
            vmem((HEADS, tokens, tokens), BF16),
            vmem((tokens, WIDTH), F32),
            vmem((tokens, WIDTH), F32),
            vmem((tokens, WIDTH), F32),
            vmem((tokens, WIDTH), F32),
            vmem((tokens, WIDTH), BF16),
            vmem((tokens, WIDTH), F32),
            vmem((HEADS, HEAD, HEAD), BF16),
            vmem((tokens, WIDTH), F32),
            vmem((tokens, WIDTH), F32),
            vmem((tokens, WIDTH), BF16),
            vmem((HEADS, 1, HEAD), F32),
        ]
        + scan_buffers
        + scan_buffers
        + [
            vmem((X, Y_HI * rows_out, WIDTH), F32),
            vmem((X, Y_HI * rows_out, WIDTH), BF16),
            vmem((X, Y_HI * rows_out, WIDTH), BF16),
            vmem((X - 1, Y_HI * rows_out, WIDTH), BF16),
            vmem((X - 1, Y_HI * rows_out, WIDTH), BF16),
            vmem((RING_Y, Z, WIDTH), F32),
            vmem((RING_Y, Z, WIDTH), BF16),
            vmem((RING_Y - 1, Z, WIDTH), BF16),
            vmem((Z, 1, WIDTH), F32),
            vmem((Z - 1, 1, WIDTH), F32),
        ]
        + [dma((1,))]
        + [dma((Z - 1,))] * 2
        + [dma((Y_LO - 1,))] * 2
        + [dma((Y_LO * (X - 1),))] * 2
        + [dma((Y_LO * X,))] * 2
        + scan_sems
        + scan_sems
        + [dma((X,))] * 2
        + [dma((X - 1,))] * 2
        + [dma((RING_Y - 1,))] * 2
        + [dma((Z - 1,))] * 2
    )
    space = pl.BlockSpec(memory_space=pltpu.VMEM)
    shape = jax.ShapeDtypeStruct
    outs = pl.pallas_call(
        body,
        out_shape=(
            shape((tokens, WIDTH), BF16),
            shape((tokens, model), BF16),
            shape((tokens, WIDTH), BF16),
            shape((tokens, WIDTH), BF16),
            shape((1, WIDTH), F32),
        ),
        in_specs=[space] * 8,
        out_specs=(space,) * 5,
        scratch_shapes=scratch,
        compiler_params=pltpu.CompilerParams(
            collective_id=0, has_side_effects=True, vmem_limit_bytes=56 * 1024 * 1024
        ),
    )(
        inputs[0],
        queries[0],
        values[0],
        w_key,
        state_in[0],
        norm_in[0],
        out_gain[None],
        out_grad[0],
    )
    return (outs[0][None], outs[1][None], outs[2][None], outs[3][None], outs[4])


def solution(mesh):
    return jax.shard_map(
        shards,
        mesh=mesh,
        in_specs=(
            P("zero", "seq", None),
            P("zero", "seq", None),
            P("zero", "seq", None),
            P("zero", None),
            P("zero", None, None, None),
            P("zero", None, None),
            P(),
            P("zero", "seq", None),
        ),
        out_specs=(
            P("zero", "seq", None),
            P("zero", "seq", None),
            P("zero", "seq", None),
            P("zero", "seq", None),
            P(("seq", "zero"), None),
        ),
        check_vma=False,
    )
```

time: 917 us -> 98.1 us (0.11)
  waiting for transfers between devices: 498 us -> 0 us
  blocking collectives: 349 us -> 0 us
  Pallas kernels: 0 us -> 92 us
  other arithmetic: 34.3 us -> 0 us
  between operations: 14.1 us -> 0.66 us
  matrix products: 10.9 us -> 0 us
    all_gather x3 -> x0, waiting for transfers between devices: 401 us -> none  [the longest x1 308 us: shards(): full_key = lax.all_gather(w_key, 'zero', axis=0, tiled=True)]
    unnamed x1 -> x0, blocking collectives: 298 us -> none
    unnamed x5 -> x0, waiting for transfers between devices: 97.1 us -> none
    pallas_call x0 -> x1, Pallas kernels: none -> 92 us  [shards(): pl.pallas_call(body, out_shape=(shape((tokens, WIDTH), BF16), shape((toke...]
    all_gather x2 -> x0, blocking collectives: 50.8 us -> none  [the longest x1 26.6 us: entering_2(): lax.all_gather(a.astype(kind), axis)]
    select_n x32 -> x0, other arithmetic: 16.9 us -> none  [turn(): return jax.tree.map(lambda a, b: jnp.where(reached, a, b), new, before)]
    add x27 -> x0, other arithmetic: 12.8 us -> none  [the longest x26 12.8 us: add_pair(): return (earlier[0] + later[0], earlier[1] + later[1])]
    dot_general x17 -> x0, matrix products: 10.9 us -> none  [the longest x1 2.54 us: shards(): key_lin = jnp.dot(token_rows, full_key, preferred_element_type=jnp.float32)]
  transfers between devices with their start and end apart: 4 -> 0, of which waited for: 4 -> 0; matrix products, arithmetic and copies ran while one was open for 1% -> 0% of each run, Pallas kernels for 0% -> 0%
where the time goes in v1:
time: 98.1 us; the launch traced here: 97.8 us
  Pallas kernels  92 us (94%)
  local copies, waits for them, and re-layouts  5.15 us (5%)
    pallas_call x1, Pallas kernels, shards(): pl.pallas_call(body, out_shape=(shape((tokens, WIDTH), BF16), shape((toke...  92 us
    unnamed x13, local copies, waits for them, and re-layouts  5.15 us

profile of v1, /device:TPU:2, one launch (start us, length us, event | category | flops | bytes accessed | tf_op | source)
XLA Modules:
  0.0 97.8 jit_solution(4018299023821548812)
XLA Ops:
  0.6 92.0 %shard_map.119 = (bf16[256,512]{1,0:T(8,128)(2,1)}, bf16[256,1024]{1,0:T(8,128)(2,1)}, bf16[256,512]{1,0:T(8,128)(2,1)}, bf16[256,512]{1,0:T(8,128)(2,1)}, f32[1,512]{1,0:T(1,128)}) custom-call(bf16[256,1024]{1,0:T(8,128)(2,1)} %bitcast.11, bf16[256,512]{1,0:T(8,128)(2,1)} %bitcast.13, bf16[256,512]{1,0:T(8,128)(2,1)} %bitcast.14, bf16[16,512]{1,0:T(8,128)(2,1)} %w.1, ...), custom_call_target="tpu_custom_call" | custom-call | tf_op jit(solution)/shard_map/pallas_call | solution.py:535
  92.7 0.0 copy-start
  92.7 1.7 %copy.18 = bf16[1,256,512]{2,1,0:T(8,128)(2,1)} copy(bf16[1,256,512]{2,1,0:T(8,128)(2,1)} %bitcast.19) | data formatting | bytes 524288
  94.4 0.0 copy-done
  94.4 0.0 copy-start.2
  94.4 0.8 copy.19
  95.2 0.3 copy-done.2
  95.5 0.0 copy-start.1
  95.5 0.7 copy.20
  96.2 0.3 copy-done.1
  96.5 0.0 copy-start.3
  96.5 0.7 copy.21
  97.2 0.0 copy-done.3
  97.2 0.6 copy.22
Async XLA Ops:
  92.7 1.7 %copy-start = (bf16[256,1024]{1,0:T(8,128)(2,1)S(1)}, bf16[256,1024]{1,0:T(8,128)(2,1)}, u32[]{:S(2)}) copy-start(bf16[256,1024]{1,0:T(8,128)(2,1)} %get-tuple-element.11) | copy-start | bytes 1572868
  94.4 1.1 %copy-start.2 = (bf16[256,512]{1,0:T(8,128)(2,1)S(1)}, bf16[256,512]{1,0:T(8,128)(2,1)}, u32[]{:S(2)}) copy-start(bf16[256,512]{1,0:T(8,128)(2,1)} %get-tuple-element.12) | copy-start | bytes 786436
  95.5 1.0 %copy-start.1 = (bf16[256,512]{1,0:T(8,128)(2,1)S(1)}, bf16[256,512]{1,0:T(8,128)(2,1)}, u32[]{:S(2)}) copy-start(bf16[256,512]{1,0:T(8,128)(2,1)} %get-tuple-element.13) | copy-start | bytes 786436
  96.5 0.7 copy-start.3

commit v2 on v1

--- a/solution.py
+++ b/solution.py
@@ -41,17 +41,18 @@
 
 
 def body(
-    inp, q, v, w, st, nm, gain, og,
+    inp_hbm, q_hbm, v_hbm, w, st_hbm, nm_hbm, gain_hbm, og_hbm,
     att, ig, qg, vg, wg,
+    inp, q, v, st, nm, gain, og,
     wf, inpt, fq, slq, fk, slk, wts, numi, deni, ho, rec, gn, gd, state, dfk, dval, dk, norm,
     f_out, f_in, f_tot, f_tot_in, f_pre, f_ret,
     b_out, b_in, b_tot, b_tot_in, b_pre, b_ret,
-    gown, gsend, grecv, xsend, xrecv, ykeep, ysend, yrecv, zsend, zrecv,
-    local_sem,
+    gown, gsend, grecv, vsend, vrecv, xsend, xrecv, ykeep, ysend, yrecv, zsend, zrecv,
+    local_sem, load_sem,
     wz_s, wz_r, wy_s, wy_r, wx_s, wx_r, wc_s, wc_r,
     fa_s, fa_r, fy_s, fy_r, fb_s, fb_r,
     ba_s, ba_r, by_s, by_r, bb_s, bb_r,
-    rc_s, rc_r, rx_s, rx_r, ry_s, ry_r, rz_s, rz_r,
+    rc_s, rc_r, rv_s, rv_r, rx_s, rx_r, ry_s, ry_r, rz_s, rz_r,
 ):
     seq, zero = lax.axis_index("seq"), lax.axis_index("zero")
     core = lax.rem(seq, CORES)
@@ -65,7 +66,9 @@
     tokens, model = inp.shape
     depth = w.shape[0]
     half = depth // CORES
-    block = WIDTH // X
+    wide_block = WIDTH // 2
+    block = wide_block // 2
+    side = lax.rem(x, 2)
 
     def send(source, target, s_sem, r_sem, to_seq, to_zero):
         return pltpu.make_async_remote_copy(
@@ -109,6 +112,17 @@
         greet(along_y(k))
     for k in range(1, GROUP):
         greet(in_group(k))
+    loads = [
+        pltpu.make_async_copy(outer, inner, load_sem.at[n])
+        for n, (outer, inner) in enumerate(
+            (
+                (inp_hbm, inp), (q_hbm, q), (v_hbm, v), (st_hbm, st),
+                (nm_hbm, nm), (gain_hbm, gain), (og_hbm, og),
+            )
+        )
+    ]
+    for load in loads:
+        load.start()
     pl.semaphore_wait(barrier, Z + RING_Y + GROUP - 3)
 
     sent = []
@@ -116,10 +130,11 @@
     def rows_of(c):
         return pl.ds(pl.multiple_of(c * half, half), half)
 
-    def columns_of(xx):
-        return pl.ds(pl.multiple_of(xx * block, block), block)
-
-    rows, columns = rows_of(core), columns_of(x)
+    def columns_of(which, quarter):
+        return pl.ds(pl.multiple_of(which * wide_block + quarter * block, block), block)
+
+    rows = rows_of(core)
+    columns = pl.ds(pl.multiple_of(side * wide_block, wide_block), wide_block)
 
     def z_copy(k):
         return send(
@@ -146,6 +161,9 @@
         w.at[rows, columns], wf.at[z, y_lo, rows, columns], local_sem.at[0]
     )
     keep.start()
+
+    for load in loads:
+        load.wait()
 
     span = CORES * Z * Y_LO
     j = lax.broadcasted_iota(jnp.int32, (span, span), 0)
@@ -172,50 +190,56 @@
 
     steps_y = [1, -1, 2 - 4 * core] if Y_LO == 4 else [1]
 
-    def piece(n, k, r):
-        lo = y_lo if n == 0 else lax.rem(y_lo - steps_y[n - 1] + 2 * Y_LO, Y_LO)
-        return wf.at[:, lo, r, columns_of(lax.rem(x - k + X, X))]
+    def source_of(n):
+        return y_lo if n == 0 else lax.rem(y_lo - steps_y[n - 1] + 2 * Y_LO, Y_LO)
 
     def y_copy(n, at):
         return send(at, at, wy_s.at[n], wy_r.at[n], *along_y(steps_y[n]))
 
-    def x_copy(n, k, at):
-        slot = n * (X - 1) + k - 1
-        return send(at, at, wx_s.at[slot], wx_r.at[slot], *along_x(k))
-
-    def c_copy(n, k, at):
-        slot = n * X + k
+    def x_copy(n, quarter, at):
+        slot = n * 2 + quarter
+        step = 1 if quarter == 0 else X - 1
+        return send(at, at, wx_s.at[slot], wx_r.at[slot], *along_x(step))
+
+    def c_copy(n, part, at):
+        slot = n * 3 + part
         return send(at, at, wc_s.at[slot], wc_r.at[slot], partner, zero)
 
+    def half_at(n, r):
+        return wf.at[:, source_of(n), r, columns]
+
+    def quarter_at(n, r, which, quarter):
+        return wf.at[:, source_of(n), r, columns_of(which, quarter)]
+
     def pass_on(n):
-        at = piece(n, 0, rows)
-        for k in (2, 1, 3) if X == 4 else range(1, X):
-            copy = x_copy(n, k, at)
+        for quarter in range(2):
+            copy = x_copy(n, quarter, quarter_at(n, rows, side, quarter))
             copy.start()
             sent.append(copy)
-        copy = c_copy(n, 0, at)
+        copy = c_copy(n, 0, half_at(n, rows))
         copy.start()
         sent.append(copy)
 
     for n in range(len(steps_y)):
-        copy = y_copy(n, piece(0, 0, rows))
+        copy = y_copy(n, half_at(0, rows))
         copy.start()
         sent.append(copy)
     pass_on(0)
     for n in range(len(steps_y)):
-        y_copy(n, piece(n + 1, 0, rows)).wait_recv()
+        y_copy(n, half_at(n + 1, rows)).wait_recv()
         pass_on(n + 1)
     for n in range(Y_LO):
-        for k in range(1, X):
-            at = piece(n, k, rows)
-            x_copy(n, k, at).wait_recv()
-            copy = c_copy(n, k, at)
+        for quarter in range(2):
+            at = quarter_at(n, rows, 1 - side, quarter)
+            x_copy(n, quarter, at).wait_recv()
+            copy = c_copy(n, 1 + quarter, at)
             copy.start()
             sent.append(copy)
     other_rows = rows_of(1 - core)
     for n in range(Y_LO):
-        for k in range(X):
-            c_copy(n, k, piece(n, k, other_rows)).wait_recv()
+        c_copy(n, 0, half_at(n, other_rows)).wait_recv()
+        for quarter in range(2):
+            c_copy(n, 1 + quarter, quarter_at(n, other_rows, 1 - side, quarter)).wait_recv()
 
     for h in range(HEADS):
         lanes = slice(h * HEAD, (h + 1) * HEAD)
@@ -303,12 +327,12 @@
         numi[:, lanes] = both[:, :HEAD]
         deni[:, lanes] = both[:, HEAD:]
 
-    for h in range(HEADS // 2):
-        inside_block(h)
+    inside_block(0)
     swap = scan_total(f_out, f_in, f_tot, f_tot_in, fa_s, fa_r, fy_s, fy_r)
-    for h in range(HEADS // 2, HEADS):
+    for h in range(1, HEADS - 1):
         inside_block(h)
     scan_back(f_in, f_tot_in, swap, y_hi, range(GROUP), f_pre, f_ret, fb_s, fb_r)
+    inside_block(HEADS - 1)
     group_wait(f_ret, fb_s, fb_r)
 
     squares = jnp.zeros((tokens, HEAD), F32)
@@ -358,10 +382,9 @@
         d_query = dot(d_weights, fk[:, lanes]) + dot_nt(grad, state[h]) + row_grad * norm[h]
         qg[:, lanes] = (d_query * slq[:, lanes]).astype(BF16)
 
-    for h in range(HEADS // 2):
-        block_grads(h)
+    block_grads(0)
     swap = scan_total(b_out, b_in, b_tot, b_tot_in, ba_s, ba_r, by_s, by_r)
-    for h in range(HEADS // 2, HEADS):
+    for h in range(1, HEADS - 1):
         block_grads(h)
     scan_back(
         b_in, b_tot_in, swap, 1 - y_hi, range(GROUP - 1, -1, -1), b_pre, b_ret, bb_s, bb_r
@@ -369,6 +392,7 @@
     for h in range(HEADS):
         lanes = slice(h * HEAD, (h + 1) * HEAD)
         att[:, lanes] = (ho[:, lanes] * inv_rms * gain[:, lanes]).astype(BF16)
+    block_grads(HEADS - 1)
     group_wait(b_ret, bb_s, bb_r)
     for h in range(HEADS):
         lanes = slice(h * HEAD, (h + 1) * HEAD)
@@ -376,35 +400,58 @@
         total = dfk[:, lanes] + dot_nt(v[:, lanes], carry) + carry_sum
         dk[:, lanes] = (total * slk[:, lanes]).astype(BF16)
 
+    rows_out = Z * Y_LO
+
     def partial_of(xx, c):
         left = jnp.concatenate([inpt[hi, xx, c] for hi in range(Y_HI)], axis=0)
         return dot(left, dk[...])
 
-    order = (2, 1, 3, 0) if X == 4 else tuple(range(1, X)) + (0,)
-
     def rc_copy(k):
         return send(gsend.at[k], grecv.at[k], rc_s.at[k], rc_r.at[k], partner, zero)
 
+    def rx_copy(slot):
+        return send(
+            xsend.at[slot], xrecv.at[slot], rx_s.at[slot], rx_r.at[slot],
+            *along_x(1 if slot == 0 else X - 1),
+        )
+
+    def relay_copy(slot):
+        return send(
+            vsend.at[slot], vrecv.at[slot], rv_s.at[slot], rv_r.at[slot],
+            *along_x(1 if slot == 0 else X - 1),
+        )
+
+    def start(copy):
+        copy.start()
+        sent.append(copy)
+
+    order = (2, 1, 3, 0)
     for k in order:
         gsend[k] = partial_of(lax.rem(x + k, X), 1 - core).astype(BF16)
-        copy = rc_copy(k)
-        copy.start()
-        sent.append(copy)
-    for k in order:
-        gown[k] = partial_of(lax.rem(x + k, X), core)
-
-    def rx_copy(k):
-        return send(
-            xsend.at[k - 1], xrecv.at[k - 1], rx_s.at[k - 1], rx_r.at[k - 1], *along_x(k)
-        )
-
-    for k in order:
+        start(rc_copy(k))
+
+    def both_cores(k):
+        mine = partial_of(lax.rem(x + k, X), core)
         rc_copy(k).wait_recv()
-        if k:
-            xsend[k - 1] = (gown[k] + wide(grecv[k])).astype(BF16)
-            copy = rx_copy(k)
-            copy.start()
-            sent.append(copy)
+        return mine + wide(grecv[k])
+
+    middle = rows_out
+    far = both_cores(2).astype(BF16)
+    vsend[0] = far[:middle]
+    start(relay_copy(0))
+    vsend[1] = far[middle:]
+    start(relay_copy(1))
+    up = both_cores(1)
+    down = both_cores(3)
+    relay_copy(0).wait_recv()
+    xsend[0, 0:middle] = (up[:middle] + wide(vrecv[0])).astype(BF16)
+    xsend[0, middle : 2 * middle] = up[middle:].astype(BF16)
+    start(rx_copy(0))
+    relay_copy(1).wait_recv()
+    xsend[1, 0:middle] = down[:middle].astype(BF16)
+    xsend[1, middle : 2 * middle] = (down[middle:] + wide(vrecv[1])).astype(BF16)
+    start(rx_copy(1))
+    gown[...] = both_cores(0)
 
     for h in range(HEADS):
         lanes = slice(h * HEAD, (h + 1) * HEAD)
@@ -412,11 +459,10 @@
         vg[:, lanes] = (dval[:, lanes] + dot(fk[:, lanes], carry)).astype(BF16)
     ig[...] = dot_nt(dk[...], wf[...].reshape(model, WIDTH)).astype(BF16)
 
-    for k in range(1, X):
-        rx_copy(k).wait_recv()
-    total = gown[0] + wide(grecv[0])
-    for k in range(1, X):
-        total = total + wide(xrecv[k - 1])
+    total = gown[...]
+    for slot in range(2):
+        rx_copy(slot).wait_recv()
+        total = total + wide(xrecv[slot])
     for there in range(RING_Y):
         part_y = total[there * Z : (there + 1) * Z]
         ykeep[there] = part_y
@@ -485,6 +531,13 @@
     scan_sems = [dma((GROUP - 1,))] * 2 + [dma((1,))] * 2 + [dma((GROUP - 1,))] * 2
     scratch = (
         [
+            vmem((tokens, model), BF16),
+            vmem((tokens, WIDTH), BF16),
+            vmem((tokens, WIDTH), BF16),
+            vmem((HEADS, HEAD, HEAD), F32),
+            vmem((HEADS, HEAD), F32),
+            vmem((1, WIDTH), F32),
+            vmem((tokens, WIDTH), BF16),
             vmem((Z, Y_LO, depth, WIDTH), BF16),
             vmem((Y_HI, X, CORES, rows_out, tokens), BF16),
             vmem((tokens, WIDTH), BF16),
@@ -507,41 +560,44 @@
         + scan_buffers
         + scan_buffers
         + [
-            vmem((X, Y_HI * rows_out, WIDTH), F32),
+            vmem((Y_HI * rows_out, WIDTH), F32),
             vmem((X, Y_HI * rows_out, WIDTH), BF16),
             vmem((X, Y_HI * rows_out, WIDTH), BF16),
-            vmem((X - 1, Y_HI * rows_out, WIDTH), BF16),
-            vmem((X - 1, Y_HI * rows_out, WIDTH), BF16),
+            vmem((2, rows_out, WIDTH), BF16),
+            vmem((2, rows_out, WIDTH), BF16),
+            vmem((2, Y_HI * rows_out, WIDTH), BF16),
+            vmem((2, Y_HI * rows_out, WIDTH), BF16),
             vmem((RING_Y, Z, WIDTH), F32),
             vmem((RING_Y, Z, WIDTH), BF16),
             vmem((RING_Y - 1, Z, WIDTH), BF16),
             vmem((Z, 1, WIDTH), F32),
             vmem((Z - 1, 1, WIDTH), F32),
         ]
-        + [dma((1,))]
+        + [dma((1,)), dma((7,))]
         + [dma((Z - 1,))] * 2
         + [dma((Y_LO - 1,))] * 2
-        + [dma((Y_LO * (X - 1),))] * 2
-        + [dma((Y_LO * X,))] * 2
+        + [dma((Y_LO * 2,))] * 2
+        + [dma((Y_LO * 3,))] * 2
         + scan_sems
         + scan_sems
         + [dma((X,))] * 2
-        + [dma((X - 1,))] * 2
+        + [dma((2,))] * 4
         + [dma((RING_Y - 1,))] * 2
         + [dma((Z - 1,))] * 2
     )
     space = pl.BlockSpec(memory_space=pltpu.VMEM)
-    shape = jax.ShapeDtypeStruct
+    anywhere = pl.BlockSpec(memory_space=pl.ANY)
+    results = (
+        ((tokens, WIDTH), BF16),
+        ((tokens, model), BF16),
+        ((tokens, WIDTH), BF16),
+        ((tokens, WIDTH), BF16),
+        ((1, WIDTH), F32),
+    )
     outs = pl.pallas_call(
         body,
-        out_shape=(
-            shape((tokens, WIDTH), BF16),
-            shape((tokens, model), BF16),
-            shape((tokens, WIDTH), BF16),
-            shape((tokens, WIDTH), BF16),
-            shape((1, WIDTH), F32),
-        ),
-        in_specs=[space] * 8,
+        out_shape=tuple(pltpu.VMEM(*r) for r in results),
+        in_specs=[anywhere] * 8,
         out_specs=(space,) * 5,
         scratch_shapes=scratch,
         compiler_params=pltpu.CompilerParams(

time: 98.1 us -> 95 us (0.968)
  the two profiles are of different devices: /device:TPU:2 before, /device:TPU:4 now
where the time goes in v2:
time: 95 us; the launch traced here: 94.9 us
  Pallas kernels  90.7 us (95%)
  local copies, waits for them, and re-layouts  3.48 us (4%)
    pallas_call x1, Pallas kernels, shards(): pl.pallas_call(body, out_shape=tuple((pltpu.VMEM(*r) for r in results)),...  90.7 us
    unnamed x5, local copies, waits for them, and re-layouts  3.48 us

profile of v2, /device:TPU:4, one launch (start us, length us, event | category | flops | bytes accessed | tf_op | source)
XLA Modules:
  0.0 94.9 jit_solution(4677570276227416589)
XLA Ops:
  0.6 90.7 %shard_map.119 = (bf16[256,512]{1,0:T(8,128)(2,1)S(1)}, bf16[256,1024]{1,0:T(8,128)(2,1)S(1)}, bf16[256,512]{1,0:T(8,128)(2,1)S(1)}, bf16[256,512]{1,0:T(8,128)(2,1)S(1)}, f32[1,512]{1,0:T(1,128)S(1)}) custom-call(bf16[256,1024]{1,0:T(8,128)(2,1)} %bitcast.15, bf16[256,512]{1,0:T(8,128)(2,1)} %bitcast.16, bf16[256,512]{1,0:T(8,128)(2,1)} %bitcast.17, ...), custom_call_target="tpu_custom_call" | custom-call | tf_op jit(solution)/shard_map/pallas_call | solution.py:597
  91.4 0.7 copy.18
  92.1 0.8 copy.19
  92.9 0.6 copy.22
  93.4 0.7 copy.20
  94.1 0.7 copy.21

commit v3 on v2

--- a/solution.py
+++ b/solution.py
@@ -42,7 +42,7 @@
 
 def body(
     inp_hbm, q_hbm, v_hbm, w, st_hbm, nm_hbm, gain_hbm, og_hbm,
-    att, ig, qg, vg, wg,
+    big, ig, wg,
     inp, q, v, st, nm, gain, og,
     wf, inpt, fq, slq, fk, slk, wts, numi, deni, ho, rec, gn, gd, state, dfk, dval, dk, norm,
     f_out, f_in, f_tot, f_tot_in, f_pre, f_ret,
@@ -54,6 +54,7 @@
     ba_s, ba_r, by_s, by_r, bb_s, bb_r,
     rc_s, rc_r, rv_s, rv_r, rx_s, rx_r, ry_s, ry_r, rz_s, rz_r,
 ):
+    att, qg, vg = big.at[0], big.at[1], big.at[2]
     seq, zero = lax.axis_index("seq"), lax.axis_index("zero")
     core = lax.rem(seq, CORES)
     x = lax.rem(seq // CORES, X)
@@ -127,6 +128,11 @@
 
     sent = []
 
+    def settle():
+        for copy in sent:
+            copy.wait_send()
+        sent.clear()
+
     def rows_of(c):
         return pl.ds(pl.multiple_of(c * half, half), half)
 
@@ -201,9 +207,12 @@
         step = 1 if quarter == 0 else X - 1
         return send(at, at, wx_s.at[slot], wx_r.at[slot], *along_x(step))
 
-    def c_copy(n, part, at):
-        slot = n * 3 + part
+    def c_copy(slot, at):
         return send(at, at, wc_s.at[slot], wc_r.at[slot], partner, zero)
+
+    def other_half(n, r):
+        far_columns = pl.ds(pl.multiple_of((1 - side) * wide_block, wide_block), wide_block)
+        return wf.at[:, source_of(n), r, far_columns]
 
     def half_at(n, r):
         return wf.at[:, source_of(n), r, columns]
@@ -216,9 +225,6 @@
             copy = x_copy(n, quarter, quarter_at(n, rows, side, quarter))
             copy.start()
             sent.append(copy)
-        copy = c_copy(n, 0, half_at(n, rows))
-        copy.start()
-        sent.append(copy)
 
     for n in range(len(steps_y)):
         copy = y_copy(n, half_at(0, rows))
@@ -228,28 +234,34 @@
     for n in range(len(steps_y)):
         y_copy(n, half_at(n + 1, rows)).wait_recv()
         pass_on(n + 1)
+    other_rows = rows_of(1 - core)
+
+    def own_half(r):
+        return wf.at[:, :, r, columns]
+
+    copy = c_copy(0, own_half(rows))
+    copy.start()
+    sent.append(copy)
     for n in range(Y_LO):
         for quarter in range(2):
-            at = quarter_at(n, rows, 1 - side, quarter)
-            x_copy(n, quarter, at).wait_recv()
-            copy = c_copy(n, 1 + quarter, at)
-            copy.start()
-            sent.append(copy)
-    other_rows = rows_of(1 - core)
+            x_copy(n, quarter, quarter_at(n, rows, 1 - side, quarter)).wait_recv()
+        copy = c_copy(1 + n, other_half(n, rows))
+        copy.start()
+        sent.append(copy)
+    c_copy(0, own_half(other_rows)).wait_recv()
     for n in range(Y_LO):
-        c_copy(n, 0, half_at(n, other_rows)).wait_recv()
-        for quarter in range(2):
-            c_copy(n, 1 + quarter, quarter_at(n, other_rows, 1 - side, quarter)).wait_recv()
-
-    for h in range(HEADS):
-        lanes = slice(h * HEAD, (h + 1) * HEAD)
-        weight = wf[:, :, :, lanes].reshape(model, HEAD)
+        c_copy(1 + n, other_half(n, other_rows)).wait_recv()
+
+    for h in range(HEADS // 2):
+        lanes = slice(h * 2 * HEAD, (h + 1) * 2 * HEAD)
+        weight = wf[:, :, :, lanes].reshape(model, 2 * HEAD)
         feat, slope = features(dot(inp[...], weight))
         fk[:, lanes] = feat.astype(BF16)
         slk[:, lanes] = slope
 
     part = WIDTH // GROUP
     padded = f_out.shape[1]
+    far_group = sorted(range(1, GROUP), key=lambda k: abs(2 * k - GROUP))
 
     def scan_start(mats, sums, out, inside, s_sem, r_sem):
         per = HEAD // part if part <= HEAD else 1
@@ -260,7 +272,7 @@
                 out[slot, part:padded] = jnp.broadcast_to(sums[h], (padded - part, HEAD)).astype(
                     BF16
                 )
-        for k in range(1, GROUP):
+        for k in far_group:
             copy = send(
                 out.at[lax.rem(own + k, GROUP)], inside.at[own],
                 s_sem.at[k - 1], r_sem.at[k - 1], *in_group(k),
@@ -291,7 +303,7 @@
         for p in order:
             pre[p] = running.astype(BF16)
             running = running + wide(inside[p])
-        for k in range(1, GROUP):
+        for k in far_group:
             copy = send(
                 pre.at[lax.rem(own + k, GROUP)], ret.at[own],
                 s_sem.at[k - 1], r_sem.at[k - 1], *in_group(k),
@@ -304,7 +316,7 @@
         per = HEAD // part
         mats = [ret[h * per + p, 0:part] for p in range(per)]
         mat = mats[0] if per == 1 else jnp.concatenate(mats, axis=0)
-        return mat, wide(ret[h * per, part : part + 16])[0:1]
+        return mat, wide(ret[h * per, part : part + 8])[0:1]
 
     mats, sums = [], []
     for h in range(HEADS):
@@ -459,6 +471,13 @@
         vg[:, lanes] = (dval[:, lanes] + dot(fk[:, lanes], carry)).astype(BF16)
     ig[...] = dot_nt(dk[...], wf[...].reshape(model, WIDTH)).astype(BF16)
 
+    settle()
+
+    def z_sent(k, carry):
+        z_copy(k).wait_send()
+        return carry
+
+    lax.fori_loop(1, Z, z_sent, 0)
     total = gown[...]
     for slot in range(2):
         rx_copy(slot).wait_recv()
@@ -495,28 +514,25 @@
         return carry
 
     lax.fori_loop(0, Z - 1, rz_start, 0)
+    settle()
     last = zsend[pl.ds(z, 1)][0]
     for k in range(1, Z):
         rz_copy(k).wait_recv()
         last = last + zrecv[k - 1]
     wg[...] = last
 
-    for copy in sent:
-        copy.wait_send()
-
-    def z_sent(k, carry):
-        z_copy(k).wait_send()
+    def rz_sent(k, carry):
         rz_copy(k).wait_send()
         return carry
 
-    lax.fori_loop(1, Z, z_sent, 0)
+    lax.fori_loop(1, Z, rz_sent, 0)
 
 
 def shards(inputs, queries, values, w_key, state_in, norm_in, out_gain, out_grad):
     docs, tokens, model = inputs.shape
     depth = w_key.shape[0]
     part = WIDTH // GROUP
-    padded = part + 16
+    padded = part + 8
     rows_out = Z * Y_LO
     dma = pltpu.SemaphoreType.DMA
     vmem = pltpu.VMEM
@@ -577,7 +593,7 @@
         + [dma((Z - 1,))] * 2
         + [dma((Y_LO - 1,))] * 2
         + [dma((Y_LO * 2,))] * 2
-        + [dma((Y_LO * 3,))] * 2
+        + [dma((Y_LO + 1,))] * 2
         + scan_sems
         + scan_sems
         + [dma((X,))] * 2
@@ -588,17 +604,15 @@
     space = pl.BlockSpec(memory_space=pltpu.VMEM)
     anywhere = pl.BlockSpec(memory_space=pl.ANY)
     results = (
-        ((tokens, WIDTH), BF16),
+        ((3, tokens, WIDTH), BF16),
         ((tokens, model), BF16),
-        ((tokens, WIDTH), BF16),
-        ((tokens, WIDTH), BF16),
         ((1, WIDTH), F32),
     )
     outs = pl.pallas_call(
         body,
         out_shape=tuple(pltpu.VMEM(*r) for r in results),
         in_specs=[anywhere] * 8,
-        out_specs=(space,) * 5,
+        out_specs=(space,) * 3,
         scratch_shapes=scratch,
         compiler_params=pltpu.CompilerParams(
             collective_id=0, has_side_effects=True, vmem_limit_bytes=56 * 1024 * 1024
@@ -613,7 +627,8 @@
         out_gain[None],
         out_grad[0],
     )
-    return (outs[0][None], outs[1][None], outs[2][None], outs[3][None], outs[4])
+    big, inputs_grad, key_grad = outs
+    return (big[0:1], inputs_grad[None], big[1:2], big[2:3], key_grad)
 
 
 def solution(mesh):

time: 95 us -> 92.6 us (0.975)
  the two profiles are of different devices: /device:TPU:4 before, /device:TPU:2 now
where the time goes in v3:
time: 92.6 us; the launch traced here: 92.4 us
  Pallas kernels  89.5 us (97%)
  local copies, waits for them, and re-layouts  2.26 us (2%)
    pallas_call x1, Pallas kernels, shards(): pl.pallas_call(body, out_shape=tuple((pltpu.VMEM(*r) for r in results)),...  89.5 us

profile of v3, /device:TPU:2, one launch (start us, length us, event | category | flops | bytes accessed | tf_op | source)
XLA Modules:
  0.0 92.4 jit_solution(5095287779260620402)
XLA Ops:
  0.6 89.5 %shard_map.119 = (bf16[3,256,512]{2,1,0:T(8,128)(2,1)S(1)}, bf16[256,1024]{1,0:T(8,128)(2,1)S(1)}, f32[1,512]{1,0:T(1,128)S(1)}) custom-call(bf16[256,1024]{1,0:T(8,128)(2,1)} %bitcast.9, bf16[256,512]{1,0:T(8,128)(2,1)} %bitcast.10, bf16[256,512]{1,0:T(8,128)(2,1)} %bitcast.11, bf16[16,512]{1,0:T(8,128)(2,1)} %w.1, f32[4,128,128]{2,1,0:T(8,128)} %bitcast.12, ...), custom_call_target="tpu_custom_call" | custom-call | tf_op jit(solution)/shard_map/pallas_call | solution.py:611
  90.1 0.8 copy.15
  90.9 0.9 fusion
  91.8 0.6 copy.16

commit v4 on v3

--- a/solution.py
+++ b/solution.py
@@ -199,9 +199,6 @@
     def source_of(n):
         return y_lo if n == 0 else lax.rem(y_lo - steps_y[n - 1] + 2 * Y_LO, Y_LO)
 
-    def y_copy(n, at):
-        return send(at, at, wy_s.at[n], wy_r.at[n], *along_y(steps_y[n]))
-
     def x_copy(n, quarter, at):
         slot = n * 2 + quarter
         step = 1 if quarter == 0 else X - 1
@@ -226,14 +223,23 @@
             copy.start()
             sent.append(copy)
 
-    for n in range(len(steps_y)):
-        copy = y_copy(n, half_at(0, rows))
-        copy.start()
-        sent.append(copy)
+    def y_quarter(n, quarter, at):
+        slot = n * 2 + quarter
+        return send(at, at, wy_s.at[slot], wy_r.at[slot], *along_y(steps_y[n]))
+
+    for quarter in range(2):
+        for n in range(len(steps_y)):
+            copy = y_quarter(n, quarter, quarter_at(0, rows, side, quarter))
+            copy.start()
+            sent.append(copy)
     pass_on(0)
-    for n in range(len(steps_y)):
-        y_copy(n, half_at(n + 1, rows)).wait_recv()
-        pass_on(n + 1)
+    for quarter in range(2):
+        for n in range(len(steps_y)):
+            at = quarter_at(n + 1, rows, side, quarter)
+            y_quarter(n, quarter, at).wait_recv()
+            copy = x_copy(n + 1, quarter, at)
+            copy.start()
+            sent.append(copy)
     other_rows = rows_of(1 - core)
 
     def own_half(r):
@@ -339,12 +345,12 @@
         numi[:, lanes] = both[:, :HEAD]
         deni[:, lanes] = both[:, HEAD:]
 
-    inside_block(0)
     swap = scan_total(f_out, f_in, f_tot, f_tot_in, fa_s, fa_r, fy_s, fy_r)
-    for h in range(1, HEADS - 1):
+    for h in range(HEADS - 2):
         inside_block(h)
     scan_back(f_in, f_tot_in, swap, y_hi, range(GROUP), f_pre, f_ret, fb_s, fb_r)
-    inside_block(HEADS - 1)
+    for h in range(HEADS - 2, HEADS):
+        inside_block(h)
     group_wait(f_ret, fb_s, fb_r)
 
     squares = jnp.zeros((tokens, HEAD), F32)
@@ -394,9 +400,8 @@
         d_query = dot(d_weights, fk[:, lanes]) + dot_nt(grad, state[h]) + row_grad * norm[h]
         qg[:, lanes] = (d_query * slq[:, lanes]).astype(BF16)
 
-    block_grads(0)
     swap = scan_total(b_out, b_in, b_tot, b_tot_in, ba_s, ba_r, by_s, by_r)
-    for h in range(1, HEADS - 1):
+    for h in range(HEADS - 2):
         block_grads(h)
     scan_back(
         b_in, b_tot_in, swap, 1 - y_hi, range(GROUP - 1, -1, -1), b_pre, b_ret, bb_s, bb_r
@@ -404,7 +409,8 @@
     for h in range(HEADS):
         lanes = slice(h * HEAD, (h + 1) * HEAD)
         att[:, lanes] = (ho[:, lanes] * inv_rms * gain[:, lanes]).astype(BF16)
-    block_grads(HEADS - 1)
+    for h in range(HEADS - 2, HEADS):
+        block_grads(h)
     group_wait(b_ret, bb_s, bb_r)
     for h in range(HEADS):
         lanes = slice(h * HEAD, (h + 1) * HEAD)
@@ -591,7 +597,7 @@
         ]
         + [dma((1,)), dma((7,))]
         + [dma((Z - 1,))] * 2
-        + [dma((Y_LO - 1,))] * 2
+        + [dma((2 * Y_LO,))] * 2
         + [dma((Y_LO * 2,))] * 2
         + [dma((Y_LO + 1,))] * 2
         + scan_sems

time: 92.6 us -> 92.6 us (level)
  the two profiles are of different devices: /device:TPU:2 before, /device:TPU:8 now
where the time goes in v4:
time: 92.6 us; the launch traced here: 92.4 us
  Pallas kernels  89.5 us (97%)
  local copies, waits for them, and re-layouts  2.26 us (2%)
    pallas_call x1, Pallas kernels, shards(): pl.pallas_call(body, out_shape=tuple((pltpu.VMEM(*r) for r in results)),...  89.5 us

profile of v4, /device:TPU:8, one launch (start us, length us, event | category | flops | bytes accessed | tf_op | source)
XLA Modules:
  0.0 92.4 jit_solution(4471323461748089295)
XLA Ops:
  0.6 89.5 %shard_map.119 = (bf16[3,256,512]{2,1,0:T(8,128)(2,1)S(1)}, bf16[256,1024]{1,0:T(8,128)(2,1)S(1)}, f32[1,512]{1,0:T(1,128)S(1)}) custom-call(bf16[256,1024]{1,0:T(8,128)(2,1)} %bitcast.9, bf16[256,512]{1,0:T(8,128)(2,1)} %bitcast.10, bf16[256,512]{1,0:T(8,128)(2,1)} %bitcast.11, bf16[16,512]{1,0:T(8,128)(2,1)} %w.1, f32[4,128,128]{2,1,0:T(8,128)} %bitcast.12, ...), custom_call_target="tpu_custom_call" | custom-call | tf_op jit(solution)/shard_map/pallas_call | solution.py:617
  90.1 0.8 copy.15
  90.9 0.9 fusion
  91.8 0.6 copy.16
